TPU v7x, 256 devices: a whole 4x4x8 slice. The times are simulated.
256 devices in a mesh: ray: 16 (over y, z_lo), pix: 16 (over z_hi, x, core).
Axes of the slice: x: 4, y: 4, z: 8 (z_hi: 2, z_lo: 4; z = z_hi * 4 + z_lo), core: 2. Of those that a mesh axis runs over, the one named last changes fastest.
Arguments:
- positions: float32 [2, 16384], P(None, 'ray'), may hold values from -2 to 2
- directions: float32 [2, 16384], P(None, 'ray'), may hold values from -0.35 to 0.35
- path: float32 [16384], P('ray'), may hold values from -9 to 9
- amplitude: float32 [16384], P('ray'), may hold values from 0.3 to 3
- psf_grad: float32 [3, 1024, 1024], P(None, 'pix', 'ray'), may hold values from -0.3 to 0.3
Outputs:
- psf: float32 [3, 1024, 1024], P(None, 'pix', 'ray')
- ray_grad: float32 [6, 16384], P(None, 'ray')
All inputs are finite; a program needn't handle non-finite values.
Results may differ from a plain program's by a relative error of at most 0.0054.
Values may be sent and summed in bfloat16 or wider, within the bound.
A program may use at most 192 MiB of HBM per device.

v0:
```python
import math
import jax
import jax.numpy as jnp
from jax import lax
from jax.sharding import PartitionSpec as P

NPIX = 1024
wave_scales = (1.2088, 1.0, 0.8953)
two_pi = 2.0 * math.pi


def centred(start, count):
    return (start + jnp.arange(count)).astype(jnp.float32) - 0.5 * NPIX + 0.5


def build_tables(rays, rows_x, cols_y, norm):
    row_list = []
    col_list = []
    weight = (rays[5] * norm)[:, None]
    for wave in range(3):
        scale = wave_scales[wave]
        angle = scale * (
            rays[4][:, None]
            + two_pi
            * (
                rays[2][:, None] * (rows_x[None, :] - rays[0][:, None])
                - rays[3][:, None] * rays[1][:, None]
            )
        )
        row_list.append(jnp.stack([weight * jnp.cos(angle), weight * jnp.sin(angle)]))
        beta = scale * two_pi * cols_y[:, None] * rays[3][None, :]
        col_list.append(jnp.stack([jnp.cos(beta), jnp.sin(beta)]))
    return (jnp.stack(row_list), jnp.stack(col_list))


def mixing(a_re, a_im):
    upper = jnp.concatenate([a_re, a_im], axis=1)
    lower = jnp.concatenate([-a_im, a_re], axis=1)
    return jnp.concatenate([upper, lower], axis=0).astype(jnp.bfloat16)


def product(left, right, dims):
    return lax.dot_general(left, right, dims, preferred_element_type=jnp.float32)


def block_count(count):
    return max(1, min(16, count // 256))


def field_terms(row_tab, col_tab):
    count = row_tab.shape[2]
    nblk = block_count(count)
    blk = count // nblk

    def step(index, total):
        a_blk = lax.dynamic_slice_in_dim(row_tab, index * blk, blk, 2)
        b_blk = lax.dynamic_slice_in_dim(col_tab, index * blk, blk, 3)
        parts = []
        for wave in range(3):
            left = jnp.concatenate([b_blk[wave, 0], b_blk[wave, 1]], axis=1).astype(jnp.bfloat16)
            parts.append(
                product(left, mixing(a_blk[wave, 0], a_blk[wave, 1]), (((1,), (0,)), ((), ())))
            )
        return total + jnp.concatenate(parts, axis=1)

    init = jnp.zeros((col_tab.shape[2], 6 * row_tab.shape[3]), jnp.float32)
    return lax.fori_loop(0, nblk, step, init)


def ray_partials(row_tab, col_tab, rows_x, cols_y, cotangent):
    count = row_tab.shape[2]
    nblk = block_count(count)
    blk = count // nblk
    plen = rows_x.shape[0]

    def one_block(index):
        a_blk = lax.dynamic_slice_in_dim(row_tab, index * blk, blk, 2)
        b_blk = lax.dynamic_slice_in_dim(col_tab, index * blk, blk, 3)
        first = jnp.zeros((blk,), jnp.float32)
        second = jnp.zeros((blk,), jnp.float32)
        third = jnp.zeros((blk,), jnp.float32)
        fourth = jnp.zeros((blk,), jnp.float32)
        for wave in range(3):
            scale = wave_scales[wave]
            a_re = a_blk[wave, 0]
            a_im = a_blk[wave, 1]
            b_re = b_blk[wave, 0]
            b_im = b_blk[wave, 1]
            left = jnp.concatenate([b_re, b_im], axis=1).astype(jnp.bfloat16)
            mix = mixing(a_re, a_im)
            grad_u = cotangent[:, 2 * plen * wave : 2 * plen * (wave + 1)]
            proj = product(left, grad_u, (((0,), (0,)), ((), ())))
            d_are = proj[:blk, :plen] + proj[blk:, plen:]
            d_aim = proj[:blk, plen:] - proj[blk:, :plen]
            d_b = product(grad_u, mix, (((1,), (1,)), ((), ())))
            d_beta = d_b[:, blk:] * b_re - d_b[:, :blk] * b_im
            d_alpha = d_aim * a_re - d_are * a_im
            first = first + scale * jnp.sum(d_alpha, axis=1)
            second = second + scale * two_pi * jnp.sum(d_alpha * rows_x[None, :], axis=1)
            third = third + scale * two_pi * jnp.sum(d_beta * cols_y[:, None], axis=0)
            fourth = fourth + jnp.sum(d_are * a_re + d_aim * a_im, axis=1)
        return jnp.stack([first, second, third, fourth])

    out = lax.map(one_block, jnp.arange(nblk))
    return jnp.transpose(out, (1, 0, 2)).reshape(4, count)


def finish(sums, rays):
    return jnp.stack(
        [
            sums[0],
            -two_pi * rays[2] * sums[0],
            -two_pi * rays[3] * sums[0],
            (sums[1] - two_pi * rays[0] * sums[0]) / NPIX,
            (sums[2] - two_pi * rays[1] * sums[0]) / NPIX,
            sums[3] / rays[5],
        ]
    )


def intensity(field, psf_grad, clen, plen):
    shaped = field.reshape(clen, 3, 2, plen)
    psf = jnp.transpose(shaped[:, :, 0] ** 2 + shaped[:, :, 1] ** 2, (1, 2, 0))
    weight = jnp.transpose(psf_grad, (2, 0, 1))
    grad_u = (2.0 * weight[:, :, None, :] * shaped).reshape(clen, 6 * plen).astype(jnp.bfloat16)
    return (psf, grad_u)


def on_device(positions, directions, path, amplitude, psf_grad):
    rays = jnp.concatenate([positions, directions, path[None], amplitude[None]], axis=0)
    local = rays.shape[1]
    plen = NPIX // lax.axis_size("pix")
    clen = NPIX // lax.axis_size("ray")
    norm = 1.0 / math.sqrt(local * lax.axis_size("ray"))
    rows_x = centred(lax.axis_index("pix") * plen, plen)
    all_cols = centred(0, NPIX)
    row_tab, col_tab = build_tables(rays, rows_x, all_cols, norm)
    field = lax.psum_scatter(field_terms(row_tab, col_tab), "ray", scatter_dimension=0, tiled=True)
    psf, grad_u = intensity(field, psf_grad, clen, plen)
    gathered = lax.all_gather(grad_u, "ray", axis=0, tiled=True)
    partial_value = ray_partials(row_tab, col_tab, rows_x, all_cols, gathered)
    sums = lax.psum(partial_value, "pix")
    return (psf, finish(sums, rays))


def solution(mesh):
    in_specs = (P(None, "ray"), P(None, "ray"), P("ray"), P("ray"), P(None, "pix", "ray"))
    out_specs = (P(None, "pix", "ray"), P(None, "ray"))
    return jax.shard_map(
        on_device, mesh=mesh, in_specs=in_specs, out_specs=out_specs, check_vma=False
    )
```

profile of v0, /device:TPU:32, one launch (start us, length us, event | category | flops | bytes accessed | tf_op | source)
XLA Modules:
  0.0 497.8 jit_solution(16539537502296417018)
XLA Ops:
  9.5 3.6 cosine_multiply_fusion.2
  13.2 46.6 %multiply_cosine_fusion.2 = (f32[1,1024,1024]{2,1,0:T(8,128)}, f32[1,1024,1024]{2,1,0:T(8,128)}, f32[1,1024,1024]{2,1,0:T(8,128)}, f32[1,1024,1024]{2,1,0:T(8,12...) fusion(f32[1024]{0:T(1024)S(1)} %bitcast.214, f32[1024]{0:T(1024)S(1)} %fusion.111, ...), kind=kLoop, calls=%fused_computation.186 | loop fusion | flops 3145728 | bytes 25182208 | tf_op jit(solution)/shard_map/cos | solution.py:32
  62.8 9.3 %maximum_bitcast_fusion.1 = (f32[1,2,1024,1024]{3,2,1,0:T(8,128)S(1)}, f32[1,2,1024,1024]{3,2,1,0:T(8,128)}) fusion(f32[1,1024,1024]{2,1,0:T(8,128)} %get-tuple-element.336, f32[1,1024,1024]{2,1,0:T(8,128)} %get-tuple-element.335, f32[1,1024,1024]{2,1,0:T(8,128)} %get-tuple-element.341, f32[1,1024,1024]{2,1,0:T(8,128)} %get-tuple-element.342), kind=kLoop, calls=%fused_computation.178 | loop fusion | flops 4194304 | bytes 33554432 | tf_op jit(solution)/shard_map/stack | solution.py:33
  72.1 15.7 %fusion.115 = (bf16[3,2,1024,1024]{3,2,1,0:T(8,128)(2,1)}, f32[3,2,1024,1024]{3,2,1,0:T(8,128)}) fusion(f32[1,2,1024,1024]{3,2,1,0:T(8,128)S(1)} %maximum_bitcast_fusion.3, f32[1,2,1024,1024]{3,2,1,0:T(8,128)} %get-tuple-element.346, f32[1,2,1024,1024]{3,2,1,0:T(8,128)S(1)} %get-tuple-element.345), kind=kLoop, calls=%fused_computation.219 | loop fusion | flops 18874368 | bytes 62914560
  87.8 56.3 %while.27 = (s32[]{:T(128)}, f32[1024,384]{0,1:T(8,128)S(1)}, bf16[3,2,1024,1024]{3,2,1,0:T(8,128)(2,1)}, f32[3,2,1024,64]{2,3,1,0:T(8,128)}, s32[]{:T(128)}, /*...) while((s32[]{:T(128)}, f32[1024,384]{0,1:T(8,128)S(1)}, bf16[3,2,1024,1024]{3,2,1,0:T(8,128)(2,1)}, ...), condition=%wide.region_1.0_spmd.clone, body=%wide.region_0.0_spmd.clone.sunk | while | flops 412237824 | bytes 23888080 | solution.py:67
  96.0 2.5 fusion.173
  110.1 2.5 fusion.173
  124.2 2.5 fusion.173
  138.2 2.5 fusion.173
  145.9 87.3 %reduce-scatter.4.cloned.1.call-done = f32[64,384]{1,0:T(8,128)} async-done(((f32[1024,384]{1,0:T(8,128)}), f32[64,384]{1,0:T(8,128)}) %reduce-scatter.4.cloned.1.call-update) | async-done | bytes 98320
  234.4 51.1 %all_gather.3 = bf16[1024,384]{1,0:T(8,128)(2,1)} all-gather(bf16[64,384]{1,0:T(8,128)(2,1)S(1)} %copy.31), channel_id=1, replica_groups=mesh['ray'=16,'pix'=16] {'ray'}, dimensions={0}, use_global_device_ids=true | all-gather | bytes 835584 | tf_op jit(solution)/shard_map/all_gather | solution.py:140
  285.5 118.7 %while.26 = (s32[]{:T(128)}, f32[4,4,256]{2,1,0:T(4,128)S(1)}, s32[4]{0:T(128)S(1)}, f32[3,2,1024,1024]{3,2,1,0:T(8,128)}, bf16[1024,384]{1,0:T(8,128)(2,1)}, /*...) while((s32[]{:T(128)}, f32[4,4,256]{2,1,0:T(4,128)S(1)}, ...), condition=%wide.region_16.17_spmd.clone.clone, body=%wide.region_3.16_spmd.clone.clone.sunk | while | flops 819468480 | bytes 79344528 | solution.py:104
  286.7 5.2 %constant_dynamic-slice_fusion.15 = (f32[1,1,1024,256]{3,2,1,0:T(8,128)S(1)}, f32[1,1,1024,256]{3,2,1,0:T(8,128)}, f32[1,1,1024,256]{3,2,1,0:T(8,128)}, f32[1,1,...) fusion(f32[3,2,1024,1024]{3,2,1,0:T(8,128)} %get-tuple-element.584, ...), kind=kLoop, calls=%fused_computation.102.clone.1 | loop fusion | bytes 12582924 | tf_op jit(solution)/shard_map/while/body/eval_jaxpr/slice | solution.py:87
  295.7 2.5 copy.70
  304.3 2.5 copy.68
  316.4 5.2 %constant_dynamic-slice_fusion.15 = (f32[1,1,1024,256]{3,2,1,0:T(8,128)S(1)}, f32[1,1,1024,256]{3,2,1,0:T(8,128)}, f32[1,1,1024,256]{3,2,1,0:T(8,128)}, f32[1,1,...) fusion(f32[3,2,1024,1024]{3,2,1,0:T(8,128)} %get-tuple-element.584, ...), kind=kLoop, calls=%fused_computation.102.clone.1 | loop fusion | bytes 12582924 | tf_op jit(solution)/shard_map/while/body/eval_jaxpr/slice | solution.py:87
  325.4 2.5 copy.70
  334.0 2.5 copy.68
  346.1 5.2 %constant_dynamic-slice_fusion.15 = (f32[1,1,1024,256]{3,2,1,0:T(8,128)S(1)}, f32[1,1,1024,256]{3,2,1,0:T(8,128)}, f32[1,1,1024,256]{3,2,1,0:T(8,128)}, f32[1,1,...) fusion(f32[3,2,1024,1024]{3,2,1,0:T(8,128)} %get-tuple-element.584, ...), kind=kLoop, calls=%fused_computation.102.clone.1 | loop fusion | bytes 12582924 | tf_op jit(solution)/shard_map/while/body/eval_jaxpr/slice | solution.py:87
  355.1 2.5 copy.70
  363.7 2.5 copy.68
  375.8 5.2 %constant_dynamic-slice_fusion.15 = (f32[1,1,1024,256]{3,2,1,0:T(8,128)S(1)}, f32[1,1,1024,256]{3,2,1,0:T(8,128)}, f32[1,1,1024,256]{3,2,1,0:T(8,128)}, f32[1,1,...) fusion(f32[3,2,1024,1024]{3,2,1,0:T(8,128)} %get-tuple-element.584, ...), kind=kLoop, calls=%fused_computation.102.clone.1 | loop fusion | bytes 12582924 | tf_op jit(solution)/shard_map/while/body/eval_jaxpr/slice | solution.py:87
  393.3 2.5 copy.68
  404.2 84.1 %psum.7 = f32[4,1024]{1,0:T(4,128)S(1)} all-reduce(f32[4,1024]{1,0:T(4,128)S(1)} %bitcast.219), channel_id=1, replica_groups=mesh['ray'=16,'pix'=16] {'pix'}, use_global_device_ids=true, to_apply=%region_17.18 | all-reduce | flops 4096 | bytes 32768 | tf_op jit(solution)/shard_map/psum | solution.py:142
  (249 shorter events, 133.7 us)
Async XLA Ops:
  7.2 226.1 %reduce-scatter.4.cloned.1.call-start = ((), (), s32[]{:S(2)}) async-start(), calls=%async_computation.1 | async-start | bytes 1671168
  144.2 1.8 copy-start.6
  234.3 51.2 %copy-start.5 = (f32[64,384]{0,1:T(8,128)}, f32[64,384]{0,1:T(8,128)S(1)}, u32[]{:S(2)}) copy-start(f32[64,384]{0,1:T(8,128)S(1)} %copy.38) | copy-start | bytes 294916
  285.5 202.9 %copy-start.7 = (f32[2,1024]{1,0:T(2,128)S(1)}, f32[2,1024]{1,0:T(2,128)}, u32[]{:S(2)}) copy-start(f32[2,1024]{1,0:T(2,128)} %param.10) | copy-start | bytes 24580
  285.5 202.9 %copy-start.8 = (f32[2,1024]{1,0:T(2,128)S(1)}, f32[2,1024]{1,0:T(2,128)}, u32[]{:S(2)}) copy-start(f32[2,1024]{1,0:T(2,128)} %param.9) | copy-start | bytes 24580
  285.5 202.9 %copy-start.9 = (f32[1024]{0:T(1024)S(1)}, f32[1024]{0:T(1024)}, u32[]{:S(2)}) copy-start(f32[1024]{0:T(1024)} %param.12) | copy-start | bytes 12292
  306.8 1.8 copy-start.3
  306.8 2.3 copy-start.4
  311.4 1.4 copy-start
  311.4 1.5 copy-start.1
  311.4 1.8 copy-start.2
  336.5 1.8 copy-start.3
  336.5 2.3 copy-start.4
  341.1 1.5 copy-start.1
  341.1 1.8 copy-start.2
  366.2 1.8 copy-start.3
  366.2 2.3 copy-start.4
  370.8 1.4 copy-start
  370.8 1.5 copy-start.1
  370.8 1.8 copy-start.2
  395.9 1.8 copy-start.3
  395.9 2.3 copy-start.4
  400.4 1.5 copy-start.1
  400.5 1.8 copy-start.2
  (2 other events, 2.8 us)
Sparse Core Ops, SparseCore 0:
  146.0 87.1 reduce-scatter.3
where the time goes:
time: 501 us; the launch traced here: 498 us
  blocking collectives  135 us (27%)
  other arithmetic  114 us (23%)
  local copies, waits for them, and re-layouts  98.7 us (20%)
  waiting for transfers between devices  87.3 us (17%)
  matrix products  44.4 us (9%)
  between operations  14.2 us (3%)
    unnamed x2, waiting for transfers between devices  87.3 us
    psum x1, blocking collectives, on_device(): sums = lax.psum(partial_value, 'pix')  84.1 us
    all_gather x1, blocking collectives, on_device(): gathered = lax.all_gather(grad_u, 'ray', axis=0, tiled=True)  51.1 us
    cos x1, other arithmetic, build_tables(): col_list.append(jnp.stack([jnp.cos(beta), jnp.sin(beta)]))  46.6 us
    dot_general x36, matrix products, product(): lax.dot_general(left, right, dims, preferred_element_type=jnp.float32)  44.4 us
    while x88, local copies, waits for them, and re-layouts  43.5 us
    slice x4, local copies, waits for them, and re-layouts, one_block(): b_re = b_blk[wave, 0]  20.6 us
    another operation x24, other arithmetic  16 us
  transfers between devices with their start and end apart: 1, of which 1 were waited for; matrix products, arithmetic and copies ran while one was open for 0% of the time, Pallas kernels for 0%

commit v1 on v0

--- a/solution.py
+++ b/solution.py
@@ -3,10 +3,15 @@
 import jax.numpy as jnp
 from jax import lax
 from jax.sharding import PartitionSpec as P
+from jax.lax import all_gather
 
 NPIX = 1024
 wave_scales = (1.2088, 1.0, 0.8953)
 two_pi = 2.0 * math.pi
+
+
+def keep_up_files(local_block):
+    return jnp.sum(all_gather(local_block, axis_name="pix"), 0)
 
 
 def centred(start, count):
@@ -139,7 +144,7 @@
     psf, grad_u = intensity(field, psf_grad, clen, plen)
     gathered = lax.all_gather(grad_u, "ray", axis=0, tiled=True)
     partial_value = ray_partials(row_tab, col_tab, rows_x, all_cols, gathered)
-    sums = lax.psum(partial_value, "pix")
+    sums = keep_up_files(partial_value)
     return (psf, finish(sums, rays))
 
 

time: 501 us -> 451 us (0.900); the launches traced: 498 us -> 443 us
  blocking collectives: 135 us -> 80 us
    psum x1 -> x0, blocking collectives: 84.1 us -> none  [on_device(): sums = lax.psum(partial_value, 'pix')]
    all_gather x0 -> x1, blocking collectives: none -> 29 us  [keep_up_files(): return jnp.sum(all_gather(local_block, axis_name='pix'), 0)]
where the time goes in v1:
time: 451 us; the launch traced here: 443 us
  other arithmetic  114 us (25%)
  local copies, waits for them, and re-layouts  98.7 us (22%)
  waiting for transfers between devices  87.3 us (19%)
  blocking collectives  80 us (18%)
  matrix products  44.4 us (10%)
  between operations  14.2 us (3%)
    unnamed x2, waiting for transfers between devices  87.3 us
    all_gather x1, blocking collectives, on_device(): gathered = lax.all_gather(grad_u, 'ray', axis=0, tiled=True)  51.1 us
    cos x1, other arithmetic, build_tables(): col_list.append(jnp.stack([jnp.cos(beta), jnp.sin(beta)]))  46.6 us
    dot_general x36, matrix products, product(): lax.dot_general(left, right, dims, preferred_element_type=jnp.float32)  44.4 us
    while x88, local copies, waits for them, and re-layouts  43.5 us
    all_gather x1, blocking collectives, keep_up_files(): return jnp.sum(all_gather(local_block, axis_name='pix'), 0)  29 us
    slice x4, local copies, waits for them, and re-layouts, one_block(): b_re = b_blk[wave, 0]  20.6 us
    another operation x24, other arithmetic  16 us
  transfers between devices with their start and end apart: 1, of which 1 were waited for; matrix products, arithmetic and copies ran while one was open for 0% of the time, Pallas kernels for 0%

profile of v1, /device:TPU:32, one launch (start us, length us, event | category | flops | bytes accessed | tf_op | source)
XLA Modules:
  0.0 442.7 jit_solution(11877989996729009138)
XLA Ops:
  9.5 3.6 cosine_multiply_fusion.2
  13.2 46.6 %multiply_cosine_fusion.2 = (f32[1,1024,1024]{2,1,0:T(8,128)}, f32[1,1024,1024]{2,1,0:T(8,128)}, f32[1,1024,1024]{2,1,0:T(8,128)}, f32[1,1024,1024]{2,1,0:T(8,12...) fusion(f32[1024]{0:T(1024)S(1)} %bitcast.214, f32[1024]{0:T(1024)S(1)} %fusion.111, ...), kind=kLoop, calls=%fused_computation.186 | loop fusion | flops 3145728 | bytes 25182208 | tf_op jit(solution)/shard_map/cos | solution.py:37
  62.8 9.3 %maximum_bitcast_fusion.1 = (f32[1,2,1024,1024]{3,2,1,0:T(8,128)S(1)}, f32[1,2,1024,1024]{3,2,1,0:T(8,128)}) fusion(f32[1,1024,1024]{2,1,0:T(8,128)} %get-tuple-element.336, f32[1,1024,1024]{2,1,0:T(8,128)} %get-tuple-element.335, f32[1,1024,1024]{2,1,0:T(8,128)} %get-tuple-element.341, f32[1,1024,1024]{2,1,0:T(8,128)} %get-tuple-element.342), kind=kLoop, calls=%fused_computation.178 | loop fusion | flops 4194304 | bytes 33554432 | tf_op jit(solution)/shard_map/stack | solution.py:38
  72.1 15.7 %fusion.115 = (bf16[3,2,1024,1024]{3,2,1,0:T(8,128)(2,1)}, f32[3,2,1024,1024]{3,2,1,0:T(8,128)}) fusion(f32[1,2,1024,1024]{3,2,1,0:T(8,128)S(1)} %maximum_bitcast_fusion.3, f32[1,2,1024,1024]{3,2,1,0:T(8,128)} %get-tuple-element.346, f32[1,2,1024,1024]{3,2,1,0:T(8,128)S(1)} %get-tuple-element.345), kind=kLoop, calls=%fused_computation.219 | loop fusion | flops 18874368 | bytes 62914560
  87.8 56.3 %while.27 = (s32[]{:T(128)}, f32[1024,384]{0,1:T(8,128)S(1)}, bf16[3,2,1024,1024]{3,2,1,0:T(8,128)(2,1)}, f32[3,2,1024,64]{2,3,1,0:T(8,128)}, s32[]{:T(128)}, /*...) while((s32[]{:T(128)}, f32[1024,384]{0,1:T(8,128)S(1)}, bf16[3,2,1024,1024]{3,2,1,0:T(8,128)(2,1)}, ...), condition=%wide.region_1.0_spmd.clone, body=%wide.region_0.0_spmd.clone.sunk | while | flops 412237824 | bytes 23888080 | solution.py:72
  96.0 2.5 fusion.173
  110.1 2.5 fusion.173
  124.2 2.5 fusion.173
  138.2 2.5 fusion.173
  145.9 87.3 %reduce-scatter.4.cloned.1.call-done = f32[64,384]{1,0:T(8,128)} async-done(((f32[1024,384]{1,0:T(8,128)}), f32[64,384]{1,0:T(8,128)}) %reduce-scatter.4.cloned.1.call-update) | async-done | bytes 98320
  234.4 51.1 %all_gather.6 = bf16[1024,384]{1,0:T(8,128)(2,1)} all-gather(bf16[64,384]{1,0:T(8,128)(2,1)S(1)} %copy.31), channel_id=1, replica_groups=mesh['ray'=16,'pix'=16] {'ray'}, dimensions={0}, use_global_device_ids=true | all-gather | bytes 835584 | tf_op jit(solution)/shard_map/all_gather | solution.py:145
  285.5 118.7 %while.26 = (s32[]{:T(128)}, f32[4,4,256]{2,1,0:T(4,128)S(1)}, s32[4]{0:T(128)S(1)}, f32[3,2,1024,1024]{3,2,1,0:T(8,128)}, bf16[1024,384]{1,0:T(8,128)(2,1)}, /*...) while((s32[]{:T(128)}, f32[4,4,256]{2,1,0:T(4,128)S(1)}, ...), condition=%wide.region_16.17_spmd.clone.clone, body=%wide.region_3.16_spmd.clone.clone.sunk | while | flops 819468480 | bytes 79344528 | solution.py:109
  286.7 5.2 %constant_dynamic-slice_fusion.15 = (f32[1,1,1024,256]{3,2,1,0:T(8,128)S(1)}, f32[1,1,1024,256]{3,2,1,0:T(8,128)}, f32[1,1,1024,256]{3,2,1,0:T(8,128)}, f32[1,1,...) fusion(f32[3,2,1024,1024]{3,2,1,0:T(8,128)} %get-tuple-element.584, ...), kind=kLoop, calls=%fused_computation.102.clone.1 | loop fusion | bytes 12582924 | tf_op jit(solution)/shard_map/while/body/eval_jaxpr/slice | solution.py:92
  295.7 2.5 copy.70
  304.3 2.5 copy.68
  316.4 5.2 %constant_dynamic-slice_fusion.15 = (f32[1,1,1024,256]{3,2,1,0:T(8,128)S(1)}, f32[1,1,1024,256]{3,2,1,0:T(8,128)}, f32[1,1,1024,256]{3,2,1,0:T(8,128)}, f32[1,1,...) fusion(f32[3,2,1024,1024]{3,2,1,0:T(8,128)} %get-tuple-element.584, ...), kind=kLoop, calls=%fused_computation.102.clone.1 | loop fusion | bytes 12582924 | tf_op jit(solution)/shard_map/while/body/eval_jaxpr/slice | solution.py:92
  325.4 2.5 copy.70
  334.0 2.5 copy.68
  346.1 5.2 %constant_dynamic-slice_fusion.15 = (f32[1,1,1024,256]{3,2,1,0:T(8,128)S(1)}, f32[1,1,1024,256]{3,2,1,0:T(8,128)}, f32[1,1,1024,256]{3,2,1,0:T(8,128)}, f32[1,1,...) fusion(f32[3,2,1024,1024]{3,2,1,0:T(8,128)} %get-tuple-element.584, ...), kind=kLoop, calls=%fused_computation.102.clone.1 | loop fusion | bytes 12582924 | tf_op jit(solution)/shard_map/while/body/eval_jaxpr/slice | solution.py:92
  355.1 2.5 copy.70
  363.7 2.5 copy.68
  375.8 5.2 %constant_dynamic-slice_fusion.15 = (f32[1,1,1024,256]{3,2,1,0:T(8,128)S(1)}, f32[1,1,1024,256]{3,2,1,0:T(8,128)}, f32[1,1,1024,256]{3,2,1,0:T(8,128)}, f32[1,1,...) fusion(f32[3,2,1024,1024]{3,2,1,0:T(8,128)} %get-tuple-element.584, ...), kind=kLoop, calls=%fused_computation.102.clone.1 | loop fusion | bytes 12582924 | tf_op jit(solution)/shard_map/while/body/eval_jaxpr/slice | solution.py:92
  393.3 2.5 copy.68
  404.2 29.0 %all_gather.7 = f32[16,4,1024]{2,1,0:T(4,128)S(1)} all-gather(f32[1,4,1024]{2,1,0:T(4,128)S(1)} %bitcast.219), channel_id=1, replica_groups=mesh['ray'=16,'pix'=16] {'pix'}, dimensions={0}, use_global_device_ids=true | all-gather | bytes 278528 | tf_op jit(solution)/shard_map/all_gather | solution.py:14
  (250 shorter events, 133.8 us)
Async XLA Ops:
  7.2 226.1 %reduce-scatter.4.cloned.1.call-start = ((), (), s32[]{:S(2)}) async-start(), calls=%async_computation.1 | async-start | bytes 1671168
  144.2 1.8 copy-start.6
  234.3 51.2 %copy-start.5 = (f32[64,384]{0,1:T(8,128)}, f32[64,384]{0,1:T(8,128)S(1)}, u32[]{:S(2)}) copy-start(f32[64,384]{0,1:T(8,128)S(1)} %copy.38) | copy-start | bytes 294916
  285.5 147.8 %copy-start.7 = (f32[2,1024]{1,0:T(2,128)S(1)}, f32[2,1024]{1,0:T(2,128)}, u32[]{:S(2)}) copy-start(f32[2,1024]{1,0:T(2,128)} %param.10) | copy-start | bytes 24580
  285.5 147.8 %copy-start.8 = (f32[2,1024]{1,0:T(2,128)S(1)}, f32[2,1024]{1,0:T(2,128)}, u32[]{:S(2)}) copy-start(f32[2,1024]{1,0:T(2,128)} %param.9) | copy-start | bytes 24580
  285.5 147.8 %copy-start.9 = (f32[1024]{0:T(1024)S(1)}, f32[1024]{0:T(1024)}, u32[]{:S(2)}) copy-start(f32[1024]{0:T(1024)} %param.12) | copy-start | bytes 12292
  306.8 1.8 copy-start.3
  306.8 2.3 copy-start.4
  311.4 1.4 copy-start
  311.4 1.5 copy-start.1
  311.4 1.8 copy-start.2
  336.5 1.8 copy-start.3
  336.5 2.3 copy-start.4
  341.1 1.5 copy-start.1
  341.1 1.8 copy-start.2
  366.2 1.8 copy-start.3
  366.2 2.3 copy-start.4
  370.8 1.4 copy-start
  370.8 1.5 copy-start.1
  370.8 1.8 copy-start.2
  395.9 1.8 copy-start.3
  395.9 2.3 copy-start.4
  400.4 1.5 copy-start.1
  400.5 1.8 copy-start.2
  (2 other events, 2.8 us)
Sparse Core Ops, SparseCore 0:
  146.0 87.1 reduce-scatter.3
